TPU v7x, 256 devices: a whole 4x4x8 slice. The times are simulated.
256 devices in a mesh: pipe: 4 (over y), tensor: 32 (over x, z_hi, core), dp: 2 (over z_lo).
Axes of the slice: x: 4, y: 4, z: 8 (z_hi: 4, z_lo: 2; z = z_hi * 2 + z_lo), core: 2. Of those that a mesh axis runs over, the one named last changes fastest.
Arguments:
- weight_main: bfloat16 [4, 4096, 2, 8192], P('pipe', None, None, 'tensor'), may hold values from -0.09375 to 0.09375
- weight_state: bfloat16 [4, 4096, 2, 1024], P('pipe', None, None, 'tensor'), may hold values from -0.09375 to 0.09375
- weight_step: bfloat16 [4, 128, 4096], P('pipe', 'tensor'), may hold values from -0.09375 to 0.09375
- weight_out: bfloat16 [4, 8192, 4096], P('pipe', 'tensor'), may hold values from -0.0625 to 0.0625
- conv_main: float32 [4, 4, 8192], P('pipe', None, 'tensor'), may hold values from -3 to 3
- conv_state: float32 [4, 4, 2, 1024], P('pipe'), may hold values from -3 to 3
- step_bias: float32 [4, 128], P('pipe', 'tensor'), may hold values from -3 to 0
- decay_log: float32 [4, 128], P('pipe', 'tensor'), may hold values from -5 to 0.5
- skip_gain: float32 [4, 128], P('pipe', 'tensor'), may hold values from 1 to 6
- norm_gain: float32 [4, 8192], P('pipe', 'tensor'), may hold values from 0.5 to 1.5
- saved_main: bfloat16 [4, 256, 2, 8192], P('pipe', 'dp', None, 'tensor'), parts along dimension 1, may hold values from -6 to 6
- saved_state: bfloat16 [4, 256, 2, 1024], P('pipe', 'dp'), parts along dimension 1, may hold values from -6 to 6
- saved_step: bfloat16 [4, 128, 256], P('pipe', 'tensor', 'dp'), parts along dimension 2, may hold values from -6 to 6
- output_grad: bfloat16 [256, 4096], P('dp', 'tensor'), parts along dimension 0, may hold values from -6 to 6
Outputs:
- input_grads: bfloat16 [4, 256, 4096], P('pipe', 'dp', 'tensor'), parts along dimension 1
There are 2 independent parts, one for each index of `dp`. A program takes and returns all parts, laid end to end along the dimension named above; an argument that names none is the same for every part. Nothing has to cross between parts.
All inputs are finite; a program needn't handle non-finite values.
Results may differ from a plain program's by a relative error of at most 0.02.
Values may be sent and summed in bfloat16 or wider, within the bound.
A program may use at most 64 MiB of HBM per device.

v0:
```python
import jax
import jax.numpy as jnp
from jax import lax
from jax.sharding import PartitionSpec as P

NSTATE = 128
GROUP_SPAN = 4
STRETCH = 128
EPSILON = 1e-05
HIGHEST = lax.Precision.HIGHEST


def from_partner(value, axis, bit):
    mask = 2**bit
    pairs = [(source, source ^ mask) for source in range(lax.axis_size(axis))]
    return lax.ppermute(value, axis, pairs)


def passed_along(value, axis, steps):
    count = lax.axis_size(axis)
    leading, last = (max(0, -steps), min(count, count - steps))
    return lax.ppermute(value, axis, [(source, source + steps) for source in range(leading, last)])


def causal_conv(signal, kernel):
    taps = kernel.shape[0]
    length = signal.shape[0]
    padded = jnp.pad(signal, ((taps - 1, 0), (0, 0)))
    summed = kernel[0] * padded[0:length]
    for offset in range(1, taps):
        summed = summed + kernel[offset] * padded[offset : offset + length]
    return summed


def state_space(values, step_sizes, decay_rates, inputs, readout):
    length, head_count, head_size = values.shape
    blocks = length // STRETCH
    state_width = inputs.shape[1]
    decays = (step_sizes * decay_rates[:, None]).reshape(head_count, blocks, STRETCH)
    running = jnp.cumsum(decays, axis=2)
    scaled = (values * step_sizes.T[:, :, None]).reshape(blocks, STRETCH, head_count, head_size)
    inputs_blocked = inputs.reshape(blocks, STRETCH, state_width)
    readout_blocked = readout.reshape(blocks, STRETCH, state_width)
    scores = jnp.einsum("cin,cjn->cij", readout_blocked, inputs_blocked, precision=HIGHEST)
    position = jnp.arange(STRETCH)
    causal = position[:, None] >= position[None, :]
    differ = running[:, :, :, None] - running[:, :, None, :]
    weights = jnp.where(causal, jnp.exp(jnp.where(causal, differ, 0.0)), 0.0) * scores[None]
    within = jnp.einsum("hcij,cjhp->cihp", weights, scaled, precision=HIGHEST)
    tail_decay = jnp.exp(running[:, :, -1:] - running)
    weighted = scaled * jnp.transpose(tail_decay, (1, 2, 0))[:, :, :, None]
    block_sums = jnp.einsum("cjhp,cjn->chpn", weighted, inputs_blocked, precision=HIGHEST)
    shrinks = jnp.exp(running[:, :, -1]).T

    def advance(carried, item):
        newest, shrink = item
        return (carried * shrink[:, None, None] + newest, carried)

    anchor = jnp.zeros((head_count, head_size, state_width), jnp.float32)
    _, entering = lax.scan(advance, anchor, (block_sums, shrinks))
    across = jnp.einsum("cin,chpn->cihp", readout_blocked, entering, precision=HIGHEST)
    across = across * jnp.transpose(jnp.exp(running), (1, 2, 0))[:, :, :, None]
    return (within + across).reshape(length, head_count, head_size)


def mamba_mixer(
    main_proj,
    state_proj,
    step_proj,
    conv_main,
    conv_state,
    step_bias,
    decay_log,
    skip_gain,
    norm_gain,
):
    length = main_proj.shape[0]
    head_count = step_proj.shape[0]
    gating = main_proj[:, 0]
    mixed_in = jax.nn.silu(causal_conv(main_proj[:, 1], conv_main))
    flat_state = state_proj.reshape(length, -1)
    state_conv = jax.nn.silu(
        causal_conv(flat_state, conv_state.reshape(conv_state.shape[0], -1))
    ).reshape(length, 2, -1)
    step_sizes = jax.nn.softplus(step_proj + step_bias[:, None])
    decay_rates = -jnp.exp(decay_log)
    values = mixed_in.reshape(length, head_count, -1)
    scanned = state_space(values, step_sizes, decay_rates, state_conv[:, 0], state_conv[:, 1])
    scanned = scanned + skip_gain[None, :, None] * values
    gated = scanned.reshape(length, -1) * jax.nn.silu(gating)
    inverse = lax.rsqrt(jnp.mean(gated * gated, axis=1, keepdims=True) + EPSILON)
    return gated * inverse * norm_gain


def body(
    weight_main,
    weight_state,
    weight_step,
    weight_out,
    conv_main,
    conv_state,
    step_bias,
    decay_log,
    skip_gain,
    norm_gain,
    saved_main,
    saved_state,
    saved_step,
    output_grad,
):
    sections = lax.axis_size("pipe")
    section = lax.axis_index("pipe")
    tensor_index = lax.axis_index("tensor")
    member = tensor_index % GROUP_SPAN
    group = tensor_index // GROUP_SPAN
    span_bits = GROUP_SPAN.bit_length() - 1
    length = saved_main.shape[1]
    col_count = output_grad.shape[1]
    model_width = weight_out.shape[2]
    main_cols = weight_main[0].reshape(model_width, -1)
    state_cols = weight_state[0].reshape(model_width, -1)
    step_rows = weight_step[0]
    out_rows = weight_out[0]
    state_group = lax.dynamic_slice_in_dim(saved_state[0], group * NSTATE, NSTATE, 2)
    conv_group = lax.dynamic_slice_in_dim(conv_state[0], group * NSTATE, NSTATE, 2)

    def local_mixer(first_in, second_in, third_in):
        return mamba_mixer(
            first_in,
            second_in,
            third_in,
            conv_main[0],
            conv_group,
            step_bias[0],
            decay_log[0],
            skip_gain[0],
            norm_gain[0],
        )

    _, pullback = jax.vjp(
        local_mixer,
        saved_main[0].astype(jnp.float32),
        state_group.astype(jnp.float32),
        saved_step[0].astype(jnp.float32),
    )
    result = jnp.zeros((length, col_count), jnp.bfloat16)
    incoming = output_grad
    for moment in range(sections):
        back_grad_main, back_grad_state, back_grad_step = pullback(
            lax.dot_general(
                lax.all_gather(incoming, "tensor", axis=1, tiled=True),
                out_rows,
                (((1,), (1,)), ((), ())),
                preferred_element_type=jnp.float32,
            )
        )
        kept = back_grad_state
        for bit in range(span_bits - 1, -1, -1):
            half = kept.shape[2] // 2
            lower = kept[:, :, :half]
            upper = kept[:, :, half:]
            high = member // 2**bit % 2 == 1
            own = jnp.where(high, upper, lower)
            other = jnp.where(high, lower, upper)
            kept = own + from_partner(other, "tensor", bit)
        grad_main = back_grad_main.astype(jnp.bfloat16).reshape(length, -1)
        grad_state = kept.astype(jnp.bfloat16).reshape(length, -1)
        grad_step = back_grad_step.astype(jnp.bfloat16)
        summed = lax.dot_general(
            main_cols, grad_main, (((1,), (1,)), ((), ())), preferred_element_type=jnp.float32
        )
        summed = summed + lax.dot_general(
            state_cols, grad_state, (((1,), (1,)), ((), ())), preferred_element_type=jnp.float32
        )
        owned = lax.psum_scatter(
            summed
            + lax.dot_general(
                step_rows, grad_step, (((0,), (0,)), ((), ())), preferred_element_type=jnp.float32
            ),
            "tensor",
            scatter_dimension=0,
            tiled=True,
        ).T.astype(jnp.bfloat16)
        result = jnp.where(section == sections - 1 - moment, owned, result)
        if moment + 1 < sections:
            incoming = passed_along(owned, "pipe", -1)
    return result[None]


def solution(mesh):
    return jax.shard_map(
        body,
        mesh=mesh,
        in_specs=(
            P("pipe", None, None, "tensor"),
            P("pipe", None, None, "tensor"),
            P("pipe", "tensor", None),
            P("pipe", "tensor", None),
            P("pipe", None, "tensor"),
            P("pipe", None, None, None),
            P("pipe", "tensor"),
            P("pipe", "tensor"),
            P("pipe", "tensor"),
            P("pipe", "tensor"),
            P("pipe", "dp", None, "tensor"),
            P("pipe", "dp", None, None),
            P("pipe", "tensor", "dp"),
            P("dp", "tensor"),
        ),
        out_specs=P("pipe", "dp", "tensor"),
        check_vma=False,
    )
```

profile of v0, /device:TPU:8, one launch (start us, length us, event | category | flops | bytes accessed | tf_op | source)
XLA Modules:
  0.0 773.3 jit_solution(89910686781437993)
XLA Ops:
  20.5 4.9 copy.113
  25.4 39.5 %all-gather.5.cloned.1.call-done = bf16[128,4096]{1,0:T(8,128)(2,1)} async-done(((bf16[128,128]{1,0:T(8,128)(2,1)}), bf16[128,4096]{1,0:T(8,128)(2,1)}) %all-gather.5.cloned.1.call-update) | async-done | bytes 1048592 | tf_op jit(solution)/shard_map/all_gather | solution.py:151
  64.9 2.1 multiply_reduce_fusion.13
  69.2 2.3 fusion.49
  72.1 2.8 fusion.63
  74.9 1.7 copy.58
  76.5 1.8 broadcast_multiply_fusion.31
  88.5 1.7 copy.60
  90.2 5.2 fusion.193
  98.2 2.5 reduce_window_sum.50
  101.6 2.0 convolution_add_fusion.7
  103.7 1.9 fusion.3
  105.7 89.8 %reduce-scatter.5.cloned.1.call-done = f32[128,128]{0,1:T(8,128)} async-done(((f32[4096,128]{0,1:T(8,128)}), f32[128,128]{0,1:T(8,128)}) %reduce-scatter.5.cloned.1.call-update) | async-done | bytes 65552 | tf_op jit(solution)/shard_map/reduce_scatter | solution.py:175
  196.3 2.4 collective-permute-start.2
  198.8 3.5 collective-permute-done.2
  202.5 49.6 %all-gather.7.cloned.1.call-done = bf16[128,4096]{1,0:T(8,128)(2,1)} async-done(((bf16[128,128]{1,0:T(8,128)(2,1)}), bf16[128,4096]{1,0:T(8,128)(2,1)}) %all-gather.7.cloned.1.call-update) | async-done | bytes 1048592 | tf_op jit(solution)/shard_map/all_gather | solution.py:151
  252.1 2.2 multiply_reduce_fusion.9
  258.1 2.3 fusion.51
  260.5 2.8 fusion.62
  278.0 1.7 copy.73
  283.1 1.7 copy.75
  284.8 5.2 fusion.194
  292.8 2.5 reduce_window_sum.52
  296.2 2.1 convolution_add_fusion.5
  298.3 1.9 fusion.2
  300.3 90.0 %reduce-scatter.7.cloned.1.call-done = f32[128,128]{0,1:T(8,128)} async-done(((f32[4096,128]{0,1:T(8,128)}), f32[128,128]{0,1:T(8,128)}) %reduce-scatter.7.cloned.1.call-update) | async-done | bytes 65552 | tf_op jit(solution)/shard_map/reduce_scatter | solution.py:175
  391.1 2.4 collective-permute-start.5
  393.6 3.5 collective-permute-done.5
  397.1 49.8 %all-gather.9.cloned.1.call-done = bf16[128,4096]{1,0:T(8,128)(2,1)} async-done(((bf16[128,128]{1,0:T(8,128)(2,1)}), bf16[128,4096]{1,0:T(8,128)(2,1)}) %all-gather.9.cloned.1.call-update) | async-done | bytes 1048592 | tf_op jit(solution)/shard_map/all_gather | solution.py:151
  446.9 2.2 multiply_reduce_fusion.7
  452.9 2.3 fusion.53
  455.3 2.8 fusion.61
  472.8 1.7 copy.83
  479.5 5.2 fusion.195
  487.5 2.5 reduce_window_sum.54
  490.9 2.0 convolution_add_fusion.3
  493.0 1.9 fusion.1
  495.0 89.9 %reduce-scatter.9.cloned.1.call-done = f32[128,128]{0,1:T(8,128)} async-done(((f32[4096,128]{0,1:T(8,128)}), f32[128,128]{0,1:T(8,128)}) %reduce-scatter.9.cloned.1.call-update) | async-done | bytes 65552 | tf_op jit(solution)/shard_map/reduce_scatter | solution.py:175
  585.8 2.4 collective-permute-start.8
  588.2 3.5 collective-permute-done.8
  591.8 49.8 %all-gather.11.cloned.1.call-done = bf16[128,4096]{1,0:T(8,128)(2,1)} async-done(((bf16[128,128]{1,0:T(8,128)(2,1)}), bf16[128,4096]{1,0:T(8,128)(2,1)}) %all-gather.11.cloned.1.call-update) | async-done | bytes 1048592 | tf_op jit(solution)/shard_map/all_gather | solution.py:151
  641.6 2.2 multiply_reduce_fusion.5
  647.0 2.3 fusion.55
  649.3 2.7 fusion.60
  663.3 5.1 fusion.196
  670.9 2.1 convolution_add_fusion.1
  673.0 1.9 fusion
  674.9 90.1 %reduce-scatter.11.cloned.1.call-done = f32[128,128]{0,1:T(8,128)} async-done(((f32[4096,128]{0,1:T(8,128)}), f32[128,128]{0,1:T(8,128)}) %reduce-scatter.11.cloned.1.call-update) | async-done | bytes 65552 | tf_op jit(solution)/shard_map/reduce_scatter | solution.py:175
  (343 shorter events, 103.9 us)
Async XLA Ops:
  6.5 58.3 %copy-start = (bf16[1,256,4096]{2,1,0:T(8,128)(2,1)S(1)}, bf16[1,256,4096]{2,1,0:T(8,128)(2,1)}, u32[]{:S(2)}) copy-start(bf16[1,256,4096]{2,1,0:T(8,128)(2,1)} %param.17) | copy-start | bytes 6291460
  6.5 58.3 %all-gather.5.cloned.1.call-start = ((), (), s32[]{:S(2)}) async-start(), calls=%async_computation.4 | async-start | bytes 1081344 | tf_op jit(solution)/shard_map/all_gather | solution.py:151
  7.3 188.2 %reduce-scatter.5.cloned.1.call-start = ((), (), s32[]{:S(2)}) async-start(), calls=%async_computation.5 | async-start | bytes 2162688 | tf_op jit(solution)/shard_map/reduce_scatter | solution.py:175
  8.3 8.3 %copy-start.85 = (f32[1,4]{1,0:T(1,128)S(1)}, f32[1,4]{1,0:T(1,128)}, u32[]{:S(2)}) copy-start(f32[1,4]{1,0:T(1,128)} %param.22) | copy-start | bytes 52
  10.1 7.3 copy-start.50
  11.1 56.5 %copy-start.2 = (f32[128,2,256]{2,0,1:T(8,128)}, f32[128,2,256]{2,0,1:T(8,128)S(1)}, u32[]{:S(2)}) copy-start(f32[128,2,256]{2,0,1:T(8,128)S(1)} %bitcast_convert_fusion) | copy-start | bytes 786436
  11.3 14.1 %copy-start.31 = (f32[128,256]{0,1:T(8,128)}, f32[128,256]{0,1:T(8,128)S(1)}, u32[]{:S(2)}) copy-start(f32[128,256]{0,1:T(8,128)S(1)} %copy.52) | copy-start | bytes 393220
  67.0 11.3 %copy-start.6 = (f32[128,256]{1,0:T(8,128)}, f32[128,256]{1,0:T(8,128)S(1)}, u32[]{:S(2)}) copy-start(f32[128,256]{1,0:T(8,128)S(1)} %get-tuple-element.152) | copy-start | bytes 393220
  68.4 11.2 %copy-start.25 = (f32[128,256]{1,0:T(8,128)S(1)}, f32[128,256]{1,0:T(8,128)}, u32[]{:S(2)}) copy-start(f32[128,256]{1,0:T(8,128)} %get-tuple-element.145) | copy-start | bytes 393220
  78.3 7.6 copy-start.40
  78.3 7.6 copy-start.42
  78.3 7.6 copy-start.44
  79.6 7.2 copy-start.10
  81.2 6.7 copy-start.24
  84.8 10.7 %collective-permute-start = (f32[128,2,64]{0,2,1:T(8,128)}, f32[128,2,64]{0,2,1:T(8,128)}, u32[]{:S(2)}, u32[]{:S(2)}) collective-permute-start(f32[128,2,64]{0,2,1:T(8,128)} %slice_select_fusion.3), channel_id=1, source_target_pairs={{0,4},{2,6},{4,0},{6,2},{8,12},{10,14},{12,8},{14,10},{16,20},{18,... | collective-permute-start | bytes 196616 | tf_op jit(solution)/shard_map/ppermute | solution.py:16
  90.2 7.4 copy-start.59
  90.2 7.4 copy-start.62
  90.2 7.4 copy-start.73
  90.2 7.4 copy-start.81
  90.2 11.3 %copy-start.1 = (bf16[1,4096,2,32]{1,3,2,0:T(8,128)(2,1)S(1)}, bf16[1,4096,2,32]{1,3,2,0:T(8,128)(2,1)}, u32[]{:S(2)}) copy-start(bf16[1,4096,2,32]{1,3,2,0:T(8,128)(2,1)} %param.15) | copy-start | bytes 1572868
  97.5 3.2 collective-permute-start.1
  105.7 146.4 %all-gather.7.cloned.1.call-start = ((), (), s32[]{:S(2)}) async-start(), calls=%async_computation.6 | async-start | bytes 1081344 | tf_op jit(solution)/shard_map/all_gather | solution.py:151
  196.3 5.9 collective-permute-start.2
  202.3 188.0 %reduce-scatter.7.cloned.1.call-start = ((), (), s32[]{:S(2)}) async-start(), calls=%async_computation.7 | async-start | bytes 2162688 | tf_op jit(solution)/shard_map/reduce_scatter | solution.py:175
  276.9 13.1 %collective-permute-start.3 = (f32[128,2,64]{0,2,1:T(8,128)}, f32[128,2,64]{0,2,1:T(8,128)}, u32[]{:S(2)}, u32[]{:S(2)}) collective-permute-start(f32[128,2,64]{0,2,1:T(8,128)} %slice_select_fusion.2), channel_id=1, source_target_pairs={{0,4},{2,6},{4,0},{6,2},{8,12},{10,14},{12,8},{14,10},{16,20},{18,... | collective-permute-start | bytes 196616 | tf_op jit(solution)/shard_map/ppermute | solution.py:16
  284.7 7.3 copy-start.51
  284.7 7.3 copy-start.75
  284.7 7.3 copy-start.83
  292.1 3.2 collective-permute-start.4
  300.2 146.7 %all-gather.9.cloned.1.call-start = ((), (), s32[]{:S(2)}) async-start(), calls=%async_computation.8 | async-start | bytes 1081344 | tf_op jit(solution)/shard_map/all_gather | solution.py:151
  391.1 5.9 collective-permute-start.5
  397.1 187.9 %reduce-scatter.9.cloned.1.call-start = ((), (), s32[]{:S(2)}) async-start(), calls=%async_computation.9 | async-start | bytes 2162688 | tf_op jit(solution)/shard_map/reduce_scatter | solution.py:175
  471.6 13.1 %collective-permute-start.6 = (f32[128,2,64]{0,2,1:T(8,128)}, f32[128,2,64]{0,2,1:T(8,128)}, u32[]{:S(2)}, u32[]{:S(2)}) collective-permute-start(f32[128,2,64]{0,2,1:T(8,128)} %slice_select_fusion.1), channel_id=1, source_target_pairs={{0,4},{2,6},{4,0},{6,2},{8,12},{10,14},{12,8},{14,10},{16,20},{18,... | collective-permute-start | bytes 196616 | tf_op jit(solution)/shard_map/ppermute | solution.py:16
  479.5 7.3 copy-start.52
  479.5 7.3 copy-start.76
  479.5 7.3 copy-start.84
  486.8 3.2 collective-permute-start.7
  495.0 146.6 %all-gather.11.cloned.1.call-start = ((), (), s32[]{:S(2)}) async-start(), calls=%async_computation.10 | async-start | bytes 1081344 | tf_op jit(solution)/shard_map/all_gather | solution.py:151
  585.8 5.9 collective-permute-start.8
  591.7 173.3 %reduce-scatter.11.cloned.1.call-start = ((), (), s32[]{:S(2)}) async-start(), calls=%async_computation.11 | async-start | bytes 2162688 | tf_op jit(solution)/shard_map/reduce_scatter | solution.py:175
  652.0 9.6 %copy-start.11 = (f32[128,256]{1,0:T(8,128)S(1)}, f32[128,256]{1,0:T(8,128)}, u32[]{:S(2)}) copy-start(f32[128,256]{1,0:T(8,128)} %get-tuple-element.108) | copy-start | bytes 393220
  656.9 6.2 copy-start.23
  659.4 9.0 %collective-permute-start.9 = (f32[128,2,64]{0,2,1:T(8,128)}, f32[128,2,64]{0,2,1:T(8,128)}, u32[]{:S(2)}, u32[]{:S(2)}) collective-permute-start(f32[128,2,64]{0,2,1:T(8,128)} %slice_select_fusion), channel_id=1, source_target_pairs={{0,4},{2,6},{4,0},{6,2},{8,12},{10,14},{12,8},{14,10},{16,20},{18,... | collective-permute-start | bytes 196616 | tf_op jit(solution)/shard_map/ppermute | solution.py:16
  663.3 6.1 copy-start.53
  669.3 1.5 collective-permute-start.10
  674.9 90.1 %copy-start.32 = (f32[128,128]{0,1:T(8,128)S(1)}, f32[128,128]{0,1:T(8,128)}, u32[]{:S(2)}) copy-start(f32[128,128]{0,1:T(8,128)} %reduce-scatter.5.cloned.1.call-done) | copy-start | bytes 196612
  674.9 90.1 %copy-start.33 = (f32[128,128]{0,1:T(8,128)S(1)}, f32[128,128]{0,1:T(8,128)}, u32[]{:S(2)}) copy-start(f32[128,128]{0,1:T(8,128)} %reduce-scatter.7.cloned.1.call-done) | copy-start | bytes 196612
  674.9 90.1 %copy-start.34 = (f32[128,128]{0,1:T(8,128)S(1)}, f32[128,128]{0,1:T(8,128)}, u32[]{:S(2)}) copy-start(f32[128,128]{0,1:T(8,128)} %reduce-scatter.9.cloned.1.call-done) | copy-start | bytes 196612
  (58 other events, 162.6 us)
Sparse Core Ops, SparseCore 0:
  9.8 54.9 all-gather.4
  105.8 89.6 reduce-scatter.4
  202.4 49.6 all-gather.6
  300.4 89.8 reduce-scatter.6
  397.2 49.6 all-gather.8
  495.1 89.8 reduce-scatter.8
  591.8 49.7 all-gather.10
  675.0 89.9 reduce-scatter.10
where the time goes:
time: 776 us; the launch traced here: 773 us
  waiting for transfers between devices  560 us (72%)
  matrix products  80.1 us (10%)
  other arithmetic  64 us (8%)
  local copies, waits for them, and re-layouts  42 us (5%)
  between operations  15 us (2%)
  starting transfers between devices  12.4 us (2%)
    reduce_scatter x4, waiting for transfers between devices, body(): lax.psum_scatter(summed + lax.dot_general(step_rows, grad_step, (((0,), (...  360 us
    all_gather x4, waiting for transfers between devices, body(): lax.all_gather(incoming, 'tensor', axis=1, tiled=True)  189 us
    dot_general x9, matrix products, state_space(): within = jnp.einsum('hcij,cjhp->cihp', weights, scaled, precision=HIGHEST)  21.1 us
    dot_general x4, matrix products, body(): lax.dot_general(main_cols, grad_main, (((1,), (1,)), ((), ())), preferred...  20.6 us
  transfers between devices with their start and end apart: 19, of which 11 were waited for; matrix products, arithmetic and copies ran while one was open for 9% of the time, Pallas kernels for 0%

commit v1 on v0

--- a/solution.py
+++ b/solution.py
@@ -8,6 +8,13 @@
 STRETCH = 128
 EPSILON = 1e-05
 HIGHEST = lax.Precision.HIGHEST
+
+
+def all_by_exchange(x, name, d):
+    n_dev = lax.axis_size(name)
+    shards = jnp.stack([x for _ in range(n_dev)])
+    shards = lax.all_to_all(shards, name, split_axis=0, concat_axis=0)
+    return jnp.concatenate(shards, axis=d)
 
 
 def from_partner(value, axis, bit):
@@ -148,7 +155,7 @@
     for moment in range(sections):
         back_grad_main, back_grad_state, back_grad_step = pullback(
             lax.dot_general(
-                lax.all_gather(incoming, "tensor", axis=1, tiled=True),
+                all_by_exchange(incoming, "tensor", 1),
                 out_rows,
                 (((1,), (1,)), ((), ())),
                 preferred_element_type=jnp.float32,

time: 776 us -> 722 us (0.930); the launches traced: 773 us -> 710 us
  waiting for transfers between devices: 560 us -> 374 us
  blocking collectives: 0 us -> 108 us
  starting transfers between devices: 12.4 us -> 23.4 us
  local copies, waits for them, and re-layouts: 42 us -> 50.7 us
    all_gather x4 -> x0, waiting for transfers between devices: 189 us -> none  [body(): lax.all_gather(incoming, 'tensor', axis=1, tiled=True)]
    all_to_all x0 -> x3, blocking collectives: none -> 108 us  [all_by_exchange(): shards = lax.all_to_all(shards, name, split_axis=0, concat_axis=0)]
    all_to_all x0 -> x1, waiting for transfers between devices: none -> 13.6 us  [all_by_exchange(): shards = lax.all_to_all(shards, name, split_axis=0, concat_axis=0)]
    all_to_all x0 -> x1, starting transfers between devices: none -> 11.6 us  [all_by_exchange(): shards = lax.all_to_all(shards, name, split_axis=0, concat_axis=0)]
    reduce_scatter x4, waiting for transfers between devices: 360 us -> 350 us  [body(): lax.psum_scatter(summed + lax.dot_general(step_rows, grad_step, (((0,), (...]
  transfers between devices with their start and end apart: 19 -> 16, of which waited for: 11 -> 8; matrix products, arithmetic and copies ran while one was open for 9% -> 10% of each run, Pallas kernels for 0% -> 0%
where the time goes in v1:
time: 722 us; the launch traced here: 710 us
  waiting for transfers between devices  374 us (52%)
  blocking collectives  108 us (15%)
  matrix products  79.1 us (11%)
  other arithmetic  59.3 us (8%)
  local copies, waits for them, and re-layouts  50.7 us (7%)
  starting transfers between devices  23.4 us (3%)
  between operations  15.3 us (2%)
    reduce_scatter x4, waiting for transfers between devices, body(): lax.psum_scatter(summed + lax.dot_general(step_rows, grad_step, (((0,), (...  350 us
    all_to_all x3, blocking collectives, all_by_exchange(): shards = lax.all_to_all(shards, name, split_axis=0, concat_axis=0)  108 us
    dot_general x9, matrix products, state_space(): within = jnp.einsum('hcij,cjhp->cihp', weights, scaled, precision=HIGHEST)  20.9 us
    dot_general x4, matrix products, body(): lax.dot_general(main_cols, grad_main, (((1,), (1,)), ((), ())), preferred...  20.6 us
  transfers between devices with their start and end apart: 16, of which 8 were waited for; matrix products, arithmetic and copies ran while one was open for 10% of the time, Pallas kernels for 0%

profile of v1, /device:TPU:8, one launch (start us, length us, event | category | flops | bytes accessed | tf_op | source)
XLA Modules:
  0.0 710.0 jit_solution(17282150755682162570)
XLA Ops:
  8.8 11.6 %all-to-all-start = ((bf16[32,128,128]{1,2,0:T(8,128)(2,1)}), bf16[32,128,128]{1,2,0:T(8,128)(2,1)}, u32[]{:S(2)}, u32[]{:S(2)}) async-start(bf16[32,128,128]{1,2,0:T(8,128)(2,1)} %stack.8), calls=%async_computation | async-start | bytes 2097152 | tf_op jit(solution)/shard_map/all_to_all | solution.py:16
  32.2 4.9 copy.117
  37.1 13.6 %all-to-all-done = bf16[32,128,128]{1,2,0:T(8,128)(2,1)} async-done(((bf16[32,128,128]{1,2,0:T(8,128)(2,1)}), bf16[32,128,128]{1,2,0:T(8,128)(2,1)}, u32[]{:S(2)}, u32[]{:S(2)}) %all-to-all-start) | async-done | bytes 1048608 | tf_op jit(solution)/shard_map/all_to_all | solution.py:16
  50.7 2.1 multiply_reduce_fusion.13
  54.5 2.3 fusion.49
  59.2 2.7 fusion.63
  63.0 1.8 broadcast_multiply_fusion.31
  73.4 1.7 copy.61
  75.1 5.2 fusion.193
  83.1 2.5 reduce_window_sum.50
  86.5 2.0 convolution_add_fusion.7
  88.7 2.0 fusion.3
  90.7 88.6 %reduce-scatter.5.cloned.1.call-done = f32[128,128]{0,1:T(8,128)} async-done(((f32[4096,128]{0,1:T(8,128)}), f32[128,128]{0,1:T(8,128)}) %reduce-scatter.5.cloned.1.call-update) | async-done | bytes 65552 | tf_op jit(solution)/shard_map/reduce_scatter | solution.py:182
  180.1 2.6 collective-permute-start.2
  182.8 3.3 collective-permute-done.2
  188.5 36.2 %all_to_all.20 = bf16[32,128,128]{1,2,0:T(8,128)(2,1)S(1)} all-to-all(bf16[32,128,128]{1,2,0:T(8,128)(2,1)S(1)} %stack.9), channel_id=1, replica_groups=mesh['pipe'=4,'tensor'=32,'dp'=2] {'tensor'}, dimensions={0} | all-to-all | bytes 2097152 | tf_op jit(solution)/shard_map/all_to_all | solution.py:16
  224.7 1.7 multiply_reduce_fusion.9
  228.9 2.3 fusion.51
  231.3 2.8 fusion.62
  240.4 1.7 copy.107
  253.9 1.7 copy.77
  255.6 5.2 fusion.194
  263.6 2.5 reduce_window_sum.52
  267.0 2.0 convolution_add_fusion.5
  269.1 2.0 fusion.2
  271.1 87.2 %reduce-scatter.7.cloned.1.call-done = f32[128,128]{0,1:T(8,128)} async-done(((f32[4096,128]{0,1:T(8,128)}), f32[128,128]{0,1:T(8,128)}) %reduce-scatter.7.cloned.1.call-update) | async-done | bytes 65552 | tf_op jit(solution)/shard_map/reduce_scatter | solution.py:182
  359.2 2.4 collective-permute-start.5
  361.6 3.5 collective-permute-done.5
  367.6 36.1 %all_to_all.21 = bf16[32,128,128]{1,2,0:T(8,128)(2,1)S(1)} all-to-all(bf16[32,128,128]{1,2,0:T(8,128)(2,1)S(1)} %stack.10), channel_id=1, replica_groups=mesh['pipe'=4,'tensor'=32,'dp'=2] {'tensor'}, dimensions={0} | all-to-all | bytes 2097152 | tf_op jit(solution)/shard_map/all_to_all | solution.py:16
  407.9 2.3 fusion.53
  410.2 2.8 fusion.61
  419.4 1.7 copy.108
  433.1 1.7 copy.88
  434.8 5.2 fusion.195
  442.8 2.5 reduce_window_sum.54
  446.2 2.0 convolution_add_fusion.3
  448.3 2.0 fusion.1
  450.4 87.0 %reduce-scatter.9.cloned.1.call-done = f32[128,128]{0,1:T(8,128)} async-done(((f32[4096,128]{0,1:T(8,128)}), f32[128,128]{0,1:T(8,128)}) %reduce-scatter.9.cloned.1.call-update) | async-done | bytes 65552 | tf_op jit(solution)/shard_map/reduce_scatter | solution.py:182
  538.2 2.5 collective-permute-start.8
  540.7 3.4 collective-permute-done.8
  546.6 36.1 %all_to_all.22 = bf16[32,128,128]{1,2,0:T(8,128)(2,1)S(1)} all-to-all(bf16[32,128,128]{1,2,0:T(8,128)(2,1)S(1)} %stack.11), channel_id=1, replica_groups=mesh['pipe'=4,'tensor'=32,'dp'=2] {'tensor'}, dimensions={0} | all-to-all | bytes 2097152 | tf_op jit(solution)/shard_map/all_to_all | solution.py:16
  582.7 1.7 multiply_reduce_fusion.5
  586.3 2.3 fusion.55
  588.6 2.7 fusion.60
  602.8 5.1 fusion.196
  610.3 2.1 convolution_add_fusion.1
  612.4 1.9 fusion
  614.4 87.2 %reduce-scatter.11.cloned.1.call-done = f32[128,128]{0,1:T(8,128)} async-done(((f32[4096,128]{0,1:T(8,128)}), f32[128,128]{0,1:T(8,128)}) %reduce-scatter.11.cloned.1.call-update) | async-done | bytes 65552 | tf_op jit(solution)/shard_map/reduce_scatter | solution.py:182
  (360 shorter events, 108.7 us)
Async XLA Ops:
  6.5 44.2 %copy-start = (bf16[1,256,4096]{2,1,0:T(8,128)(2,1)S(1)}, bf16[1,256,4096]{2,1,0:T(8,128)(2,1)}, u32[]{:S(2)}) copy-start(bf16[1,256,4096]{2,1,0:T(8,128)(2,1)} %param.17) | copy-start | bytes 6291460
  7.6 14.8 %copy-start.81 = (f32[1,4,256]{2,1,0:T(4,128)S(1)}, f32[1,4,256]{2,1,0:T(4,128)}, u32[]{:S(2)}) copy-start(f32[1,4,256]{2,1,0:T(4,128)} %param.18) | copy-start | bytes 12292
  7.6 15.2 %copy-start.35 = (bf16[1,128,2,256]{3,2,1,0:T(2,128)(2,1)S(1)}, bf16[1,128,2,256]{3,2,1,0:T(2,128)(2,1)}, u32[]{:S(2)}) copy-start(bf16[1,128,2,256]{3,2,1,0:T(2,128)(2,1)} %param.24) | copy-start | bytes 393220
  8.8 14.2 %copy-start.94 = (f32[1,4]{1,0:T(1,128)S(1)}, f32[1,4]{1,0:T(1,128)}, u32[]{:S(2)}) copy-start(f32[1,4]{1,0:T(1,128)} %param.21) | copy-start | bytes 52
  8.8 14.3 %copy-start.46 = (bf16[1,4,128]{2,1,0:T(4,128)(2,1)S(1)}, bf16[1,4,128]{2,1,0:T(4,128)(2,1)}, u32[]{:S(2)}) copy-start(bf16[1,4,128]{2,1,0:T(4,128)(2,1)} %param.26) | copy-start | bytes 3076
  8.8 14.3 %copy-start.55 = (f32[1,4]{1,0:T(1,128)S(1)}, f32[1,4]{1,0:T(1,128)}, u32[]{:S(2)}) copy-start(f32[1,4]{1,0:T(1,128)} %param.20) | copy-start | bytes 52
  8.8 41.9 %all-to-all-start = ((bf16[32,128,128]{1,2,0:T(8,128)(2,1)}), bf16[32,128,128]{1,2,0:T(8,128)(2,1)}, u32[]{:S(2)}, u32[]{:S(2)}) async-start(bf16[32,128,128]{1,2,0:T(8,128)(2,1)} %stack.8), calls=%async_computation | async-start | bytes 2097152 | tf_op jit(solution)/shard_map/all_to_all | solution.py:16
  20.4 158.9 %reduce-scatter.5.cloned.1.call-start = ((), (), s32[]{:S(2)}) async-start(), calls=%async_computation.8 | async-start | bytes 2162688 | tf_op jit(solution)/shard_map/reduce_scatter | solution.py:182
  21.4 6.9 copy-start.90
  22.8 6.4 copy-start.51
  22.8 30.7 %copy-start.2 = (f32[128,2,256]{2,0,1:T(8,128)}, f32[128,2,256]{2,0,1:T(8,128)S(1)}, u32[]{:S(2)}) copy-start(f32[128,2,256]{2,0,1:T(8,128)S(1)} %bitcast_convert_fusion) | copy-start | bytes 786436
  23.1 14.0 %copy-start.31 = (f32[128,256]{0,1:T(8,128)}, f32[128,256]{0,1:T(8,128)S(1)}, u32[]{:S(2)}) copy-start(f32[128,256]{0,1:T(8,128)S(1)} %copy.53) | copy-start | bytes 393220
  52.9 11.9 %copy-start.6 = (f32[128,256]{1,0:T(8,128)}, f32[128,256]{1,0:T(8,128)S(1)}, u32[]{:S(2)}) copy-start(f32[128,256]{1,0:T(8,128)S(1)} %get-tuple-element.152) | copy-start | bytes 393220
  54.4 11.3 %copy-start.27 = (f32[128,256]{0,1:T(8,128)}, f32[128,256]{0,1:T(8,128)S(1)}, u32[]{:S(2)}) copy-start(f32[128,256]{0,1:T(8,128)S(1)} %copy.58) | copy-start | bytes 393220
  66.1 6.6 copy-start.10
  70.8 9.6 %collective-permute-start = (f32[128,2,64]{0,2,1:T(8,128)}, f32[128,2,64]{0,2,1:T(8,128)}, u32[]{:S(2)}, u32[]{:S(2)}) collective-permute-start(f32[128,2,64]{0,2,1:T(8,128)} %slice_select_fusion.3), channel_id=1, source_target_pairs={{0,4},{2,6},{4,0},{6,2},{8,12},{10,14},{12,8},{14,10},{16,20},{18,... | collective-permute-start | bytes 196616 | tf_op jit(solution)/shard_map/ppermute | solution.py:23
  75.0 7.4 %copy-start.60 = (f32[4,1,128]{2,1,0:T(1,128)S(1)}, f32[4,1,128]{2,1,0:T(1,128)}, u32[]{:S(2)}) copy-start(f32[4,1,128]{2,1,0:T(1,128)} %get-tuple-element.142) | copy-start | bytes 6148
  75.1 7.4 %copy-start.63 = (f32[128,4]{0,1:T(4,128)S(1)}, f32[128,4]{0,1:T(4,128)}, u32[]{:S(2)}) copy-start(f32[128,4]{0,1:T(4,128)} %copy-done.62) | copy-start | bytes 6148
  75.1 7.4 %copy-start.77 = (f32[4,128]{1,0:T(4,128)S(1)}, f32[4,128]{1,0:T(4,128)}, u32[]{:S(2)}) copy-start(f32[4,128]{1,0:T(4,128)} %neg.67) | copy-start | bytes 6148
  75.1 7.4 %copy-start.86 = (f32[4,128]{1,0:T(4,128)S(1)}, f32[4,128]{1,0:T(4,128)}, u32[]{:S(2)}) copy-start(f32[4,128]{1,0:T(4,128)} %get-tuple-element.84) | copy-start | bytes 6148
  75.1 11.4 %copy-start.1 = (bf16[1,4096,2,32]{1,3,2,0:T(8,128)(2,1)S(1)}, bf16[1,4096,2,32]{1,3,2,0:T(8,128)(2,1)}, u32[]{:S(2)}) copy-start(bf16[1,4096,2,32]{1,3,2,0:T(8,128)(2,1)} %param.15) | copy-start | bytes 1572868
  82.4 3.2 collective-permute-start.1
  90.6 267.7 %reduce-scatter.7.cloned.1.call-start = ((), (), s32[]{:S(2)}) async-start(), calls=%async_computation.9 | async-start | bytes 2162688 | tf_op jit(solution)/shard_map/reduce_scatter | solution.py:182
  180.1 5.9 collective-permute-start.2
  247.6 13.2 %collective-permute-start.3 = (f32[128,2,64]{0,2,1:T(8,128)}, f32[128,2,64]{0,2,1:T(8,128)}, u32[]{:S(2)}, u32[]{:S(2)}) collective-permute-start(f32[128,2,64]{0,2,1:T(8,128)} %slice_select_fusion.2), channel_id=1, source_target_pairs={{0,4},{2,6},{4,0},{6,2},{8,12},{10,14},{12,8},{14,10},{16,20},{18,... | collective-permute-start | bytes 196616 | tf_op jit(solution)/shard_map/ppermute | solution.py:23
  255.6 7.3 %copy-start.52 = (f32[4,1,128]{2,1,0:T(1,128)S(1)}, f32[4,1,128]{2,1,0:T(1,128)}, u32[]{:S(2)}) copy-start(f32[4,1,128]{2,1,0:T(1,128)} %get-tuple-element.140) | copy-start | bytes 6148
  255.6 7.3 %copy-start.79 = (f32[4,128]{1,0:T(4,128)S(1)}, f32[4,128]{1,0:T(4,128)}, u32[]{:S(2)}) copy-start(f32[4,128]{1,0:T(4,128)} %neg.69) | copy-start | bytes 6148
  255.6 7.3 %copy-start.88 = (f32[4,128]{1,0:T(4,128)S(1)}, f32[4,128]{1,0:T(4,128)}, u32[]{:S(2)}) copy-start(f32[4,128]{1,0:T(4,128)} %get-tuple-element.82) | copy-start | bytes 6148
  262.9 3.2 collective-permute-start.4
  271.1 266.3 %reduce-scatter.9.cloned.1.call-start = ((), (), s32[]{:S(2)}) async-start(), calls=%async_computation.10 | async-start | bytes 2162688 | tf_op jit(solution)/shard_map/reduce_scatter | solution.py:182
  359.2 5.9 collective-permute-start.5
  426.6 13.5 %collective-permute-start.6 = (f32[128,2,64]{0,2,1:T(8,128)}, f32[128,2,64]{0,2,1:T(8,128)}, u32[]{:S(2)}, u32[]{:S(2)}) collective-permute-start(f32[128,2,64]{0,2,1:T(8,128)} %slice_select_fusion.1), channel_id=1, source_target_pairs={{0,4},{2,6},{4,0},{6,2},{8,12},{10,14},{12,8},{14,10},{16,20},{18,... | collective-permute-start | bytes 196616 | tf_op jit(solution)/shard_map/ppermute | solution.py:23
  434.8 7.3 %copy-start.53 = (f32[4,1,128]{2,1,0:T(1,128)S(1)}, f32[4,1,128]{2,1,0:T(1,128)}, u32[]{:S(2)}) copy-start(f32[4,1,128]{2,1,0:T(1,128)} %get-tuple-element.140) | copy-start | bytes 6148
  434.8 7.3 %copy-start.80 = (f32[4,128]{1,0:T(4,128)S(1)}, f32[4,128]{1,0:T(4,128)}, u32[]{:S(2)}) copy-start(f32[4,128]{1,0:T(4,128)} %neg.71) | copy-start | bytes 6148
  434.8 7.3 %copy-start.89 = (f32[4,128]{1,0:T(4,128)S(1)}, f32[4,128]{1,0:T(4,128)}, u32[]{:S(2)}) copy-start(f32[4,128]{1,0:T(4,128)} %get-tuple-element.80) | copy-start | bytes 6148
  442.1 3.2 collective-permute-start.7
  450.3 251.3 %reduce-scatter.11.cloned.1.call-start = ((), (), s32[]{:S(2)}) async-start(), calls=%async_computation.11 | async-start | bytes 2162688 | tf_op jit(solution)/shard_map/reduce_scatter | solution.py:182
  538.2 5.9 collective-permute-start.8
  591.3 9.7 %copy-start.11 = (f32[128,256]{1,0:T(8,128)S(1)}, f32[128,256]{1,0:T(8,128)}, u32[]{:S(2)}) copy-start(f32[128,256]{1,0:T(8,128)} %get-tuple-element.108) | copy-start | bytes 393220
  596.3 6.3 copy-start.23
  598.8 9.2 %collective-permute-start.9 = (f32[128,2,64]{0,2,1:T(8,128)}, f32[128,2,64]{0,2,1:T(8,128)}, u32[]{:S(2)}, u32[]{:S(2)}) collective-permute-start(f32[128,2,64]{0,2,1:T(8,128)} %slice_select_fusion), channel_id=1, source_target_pairs={{0,4},{2,6},{4,0},{6,2},{8,12},{10,14},{12,8},{14,10},{16,20},{18,... | collective-permute-start | bytes 196616 | tf_op jit(solution)/shard_map/ppermute | solution.py:23
  602.7 6.1 copy-start.54
  602.8 6.1 copy-start.78
  602.8 6.1 copy-start.87
  608.8 1.5 collective-permute-start.10
  614.4 87.3 %copy-start.32 = (f32[128,128]{0,1:T(8,128)S(1)}, f32[128,128]{0,1:T(8,128)}, u32[]{:S(2)}) copy-start(f32[128,128]{0,1:T(8,128)} %reduce-scatter.5.cloned.1.call-done) | copy-start | bytes 196612
  614.4 87.3 %copy-start.33 = (f32[128,128]{0,1:T(8,128)S(1)}, f32[128,128]{0,1:T(8,128)}, u32[]{:S(2)}) copy-start(f32[128,128]{0,1:T(8,128)} %reduce-scatter.7.cloned.1.call-done) | copy-start | bytes 196612
  614.4 87.3 %copy-start.34 = (f32[128,128]{0,1:T(8,128)S(1)}, f32[128,128]{0,1:T(8,128)}, u32[]{:S(2)}) copy-start(f32[128,128]{0,1:T(8,128)} %reduce-scatter.9.cloned.1.call-done) | copy-start | bytes 196612
  (63 other events, 157.9 us)
Sparse Core Ops, SparseCore 0:
  90.8 88.4 reduce-scatter.4
  271.2 87.1 reduce-scatter.6
  450.4 86.8 reduce-scatter.8
  614.5 87.0 reduce-scatter.10
